TPU v7x, 32 devices: a whole 2x2x4 slice. The times are simulated.
32 devices in a mesh: shard: 4 (over z), ctx: 4 (over x, core), tp: 2 (over y).
Axes of the slice: x: 2, y: 2, z: 4, core: 2. Of those that a mesh axis runs over, the one named last changes fastest.
Arguments:
- inputs: bfloat16 [4, 2048, 2048], P('shard', 'ctx'), may hold values from -6 to 6
- cotangent: bfloat16 [4, 2048, 2048], P('shard', 'ctx'), may hold values from -6 to 6
- query_weight: bfloat16 [2048, 2048], P('shard', 'tp'), may hold values from -0.1875 to 0.1875
- key_weight: bfloat16 [2048, 2048], P('shard', 'tp'), may hold values from -0.1875 to 0.1875
- value_weight: bfloat16 [2048, 2048], P('shard', 'tp'), may hold values from -0.125 to 0.125
- output_weight: bfloat16 [2048, 2048], P('shard', 'tp'), may hold values from -0.75 to 0.75
- up_weight: bfloat16 [2048, 8192], P('shard', 'tp'), may hold values from -0.125 to 0.125
- down_weight: bfloat16 [2048, 8192], P('shard', 'tp'), may hold values from -0.0625 to 0.0625
- query_value_bias: bfloat16 [2, 16, 128], P(None, 'tp', 'shard'), may hold values from -3 to 3
- up_bias: bfloat16 [64, 128], P('tp', 'shard'), may hold values from -3 to 3
- norm_gains: bfloat16 [2, 16, 128], P(None, 'tp', 'shard'), may hold values from 0.25 to 1.75
- other_biases: bfloat16 [4, 16, 128], P(None, 'tp', 'shard'), may hold values from -2 to 2
Outputs:
- outputs: bfloat16 [4, 2048, 2048], P('shard', 'ctx')
- input_grad: bfloat16 [4, 2048, 2048], P('shard', 'ctx')
- grad_query: float32 [2048, 2048], P('shard', 'tp')
- grad_key: float32 [2048, 2048], P('shard', 'tp')
- grad_value: float32 [2048, 2048], P('shard', 'tp')
- grad_output: float32 [2048, 2048], P('shard', 'tp')
- grad_up: float32 [2048, 8192], P('shard', 'tp')
- grad_down: float32 [2048, 8192], P('shard', 'tp')
- grad_qv_bias: float32 [2, 16, 128], P(None, 'tp', 'shard')
- grad_up_bias: float32 [64, 128], P('tp', 'shard')
- grad_gains: float32 [2, 16, 128], P(None, 'tp', 'shard')
- grad_biases: float32 [4, 16, 128], P(None, 'tp', 'shard')
- root_squares: float32 [3], replicated
All inputs are finite; a program needn't handle non-finite values.
Results may differ from a plain program's by a relative error of at most 0.024.
Values may be sent and summed in bfloat16 or wider, within the bound.
No kernel may reach another device: no remote copies, remote signals or barrier semaphores. Data moves between devices by JAX's collectives and lax.ppermute only.
A program may use at most 320 MiB of HBM per device.

v0:
```python
import jax
import jax.numpy as jnp
from jax import lax
from jax.sharding import PartitionSpec as P

D = 2048
H = 16
DH = 128
epsilon = 1e-12


def product(left, right):
    return jnp.dot(left, right, preferred_element_type=jnp.float32)


def times_transposed(left, right):
    return lax.dot_general(
        left, right, (((1,), (1,)), ((), ())), preferred_element_type=jnp.float32
    )


def transposed_times(left, right):
    return lax.dot_general(
        left, right, (((0,), (0,)), ((), ())), preferred_element_type=jnp.float32
    )


def normalize(stream):
    center = stream - jnp.mean(stream, axis=-1, keepdims=True)
    factor = lax.rsqrt(jnp.mean(center * center, axis=-1, keepdims=True) + epsilon)
    return (center * factor, factor)


def norm_backward(grad_norm, normed, factor):
    return factor * (
        grad_norm
        - jnp.mean(grad_norm, axis=-1, keepdims=True)
        - normed * jnp.mean(grad_norm * normed, axis=-1, keepdims=True)
    )


def gelu_tanh(values):
    return jax.nn.gelu(values, approximate=True)


def split_heads(matrix, heads_here):
    return matrix.reshape(matrix.shape[0], heads_here, DH).transpose(1, 0, 2)


def merge_heads(stacked):
    return stacked.transpose(1, 0, 2).reshape(stacked.shape[1], stacked.shape[0] * stacked.shape[2])


def head_forward(triple):
    q_head, k_head, v_head = triple
    scores = times_transposed(q_head, k_head) * DH ** (-0.5)
    peak = jnp.max(scores, axis=-1, keepdims=True)
    expo = jnp.exp(scores - peak)
    total = jnp.sum(expo, axis=-1, keepdims=True)
    probs = expo / total
    result = product(probs.astype(jnp.bfloat16), v_head)
    return (result, (peak + jnp.log(total))[:, 0])


def head_backward(group):
    q_head, k_head, v_head, d_head, logsum = group
    scale = DH ** (-0.5)
    scores = times_transposed(q_head, k_head) * scale
    probs = jnp.exp(scores - logsum[:, None])
    d_probs = times_transposed(d_head, v_head)
    inner = jnp.sum(probs * d_probs, axis=-1, keepdims=True)
    d_scores = (probs * (d_probs - inner)).astype(jnp.bfloat16)
    d_query = product(d_scores, k_head) * scale
    d_key = transposed_times(d_scores, q_head) * scale
    d_value = transposed_times(probs.astype(jnp.bfloat16), d_head)
    return (d_query, d_key, d_value)


def shards(
    inputs,
    cotangent,
    query_weight,
    key_weight,
    value_weight,
    output_weight,
    up_weight,
    down_weight,
    query_value_bias,
    up_bias,
    norm_gains,
    other_biases,
):
    local_rows = inputs.shape[1]
    tokens = inputs.reshape(local_rows, D)
    grad_out = cotangent.reshape(local_rows, D).astype(jnp.float32)
    gathered = (
        lax.all_gather(query_weight, "shard", axis=0, tiled=True),
        lax.all_gather(key_weight, "shard", axis=0, tiled=True),
        lax.all_gather(value_weight, "shard", axis=0, tiled=True),
        lax.all_gather(output_weight, "shard", axis=0, tiled=True),
        lax.all_gather(query_value_bias, "shard", axis=2, tiled=True),
        lax.all_gather(norm_gains, "shard", axis=2, tiled=True),
        lax.all_gather(other_biases, "shard", axis=2, tiled=True),
    )
    query_full, key_full, value_full, output_full, qv_full, gain_half, bias_half = gathered
    gain_whole, bias_whole = (
        lax.all_gather(gain_half, "tp", axis=1, tiled=True),
        lax.all_gather(bias_half, "tp", axis=1, tiled=True),
    )
    gains = gain_whole.reshape(2, D).astype(jnp.float32)
    biases = bias_whole.reshape(4, D).astype(jnp.float32)
    half_width = query_full.shape[1]
    heads_here = half_width // DH
    qv_vector = qv_full.reshape(2, half_width).astype(jnp.float32)
    queries = (product(tokens, query_full) + qv_vector[0]).astype(jnp.bfloat16)
    keys_mine = product(tokens, key_full).astype(jnp.bfloat16)
    values_mine = (product(tokens, value_full) + qv_vector[1]).astype(jnp.bfloat16)
    keys_all, values_all = (
        lax.all_gather(keys_mine, "ctx", axis=0, tiled=True),
        lax.all_gather(values_mine, "ctx", axis=0, tiled=True),
    )
    query_heads = split_heads(queries, heads_here)
    key_heads = split_heads(keys_all, heads_here)
    value_heads = split_heads(values_all, heads_here)
    head_out, logsums = lax.map(head_forward, (query_heads, key_heads, value_heads))
    attended = merge_heads(head_out).astype(jnp.bfloat16)
    attn_part = times_transposed(attended, output_full)
    attn_branch = lax.psum(attn_part.astype(jnp.bfloat16), "tp").astype(jnp.float32) + biases[0]
    normed_one, factor_one = normalize(tokens.astype(jnp.float32) + attn_branch)
    hidden_one = normed_one * gains[0] + biases[1]
    hidden_low = hidden_one.astype(jnp.bfloat16)
    up_full, down_full, up_bias_full = (
        lax.all_gather(up_weight, "shard", axis=0, tiled=True),
        lax.all_gather(down_weight, "shard", axis=0, tiled=True),
        lax.all_gather(up_bias, "shard", axis=1, tiled=True),
    )
    pre_act = product(hidden_low, up_full) + up_bias_full.reshape(-1).astype(jnp.float32)
    activated = gelu_tanh(pre_act).astype(jnp.bfloat16)
    mlp_part = times_transposed(activated, down_full)
    mlp_branch = lax.psum(mlp_part.astype(jnp.bfloat16), "tp").astype(jnp.float32) + biases[2]
    second = hidden_one + mlp_branch
    normed_two, factor_two = normalize(second)
    result = normed_two * gains[1] + biases[3]
    square_sums = jnp.stack(
        [
            jnp.sum(second * second),
            jnp.sum(attn_branch * attn_branch),
            jnp.sum(mlp_branch * mlp_branch),
        ]
    )
    grad_second = norm_backward(grad_out * gains[1], normed_two, factor_two)
    grad_mlp = grad_second.astype(jnp.bfloat16)
    grad_act = product(grad_mlp, down_full)
    unused, gelu_pull = jax.vjp(gelu_tanh, pre_act)
    grad_pre = gelu_pull(grad_act)[0].astype(jnp.bfloat16)
    hidden_part = times_transposed(grad_pre, up_full)
    grad_hidden = grad_second + lax.psum(hidden_part.astype(jnp.bfloat16), "tp").astype(jnp.float32)
    grad_first = norm_backward(grad_hidden * gains[0], normed_one, factor_one)
    grad_branch = grad_first.astype(jnp.bfloat16)
    grad_attended = product(grad_branch, output_full).astype(jnp.bfloat16)
    grad_heads = split_heads(grad_attended, heads_here)
    dq_heads, dk_heads, dv_heads = lax.map(
        head_backward, (query_heads, key_heads, value_heads, grad_heads, logsums)
    )
    grad_queries = merge_heads(dq_heads).astype(jnp.bfloat16)
    key_sums, value_sums = (
        lax.psum_scatter(
            merge_heads(dk_heads).astype(jnp.bfloat16), "ctx", scatter_dimension=0, tiled=True
        ).astype(jnp.float32),
        lax.psum_scatter(
            merge_heads(dv_heads).astype(jnp.bfloat16), "ctx", scatter_dimension=0, tiled=True
        ).astype(jnp.float32),
    )
    grad_keys = key_sums.astype(jnp.bfloat16)
    grad_values = value_sums.astype(jnp.bfloat16)
    input_part = (
        times_transposed(grad_queries, query_full)
        + times_transposed(grad_keys, key_full)
        + times_transposed(grad_values, value_full)
    )
    input_grad = grad_first + lax.psum(input_part.astype(jnp.bfloat16), "tp").astype(jnp.float32)
    qv_sums = jnp.stack(
        [
            jnp.sum(grad_queries.astype(jnp.float32), axis=0),
            jnp.sum(grad_values.astype(jnp.float32), axis=0),
        ]
    )
    up_sums = jnp.sum(grad_pre.astype(jnp.float32), axis=0)
    gain_sums = jnp.stack(
        [jnp.sum(grad_hidden * normed_one, axis=0), jnp.sum(grad_out * normed_two, axis=0)]
    )
    bias_sums = jnp.stack(
        [
            jnp.sum(grad_branch.astype(jnp.float32), axis=0),
            jnp.sum(grad_hidden, axis=0),
            jnp.sum(grad_mlp.astype(jnp.float32), axis=0),
            jnp.sum(grad_out, axis=0),
        ]
    )
    qv_total, up_total, gain_total, bias_total, square_total = lax.psum(
        (qv_sums, up_sums, gain_sums, bias_sums, square_sums), ("shard", "ctx")
    )
    summed = lax.psum_scatter(
        jnp.concatenate(
            [
                transposed_times(tokens, grad_queries),
                transposed_times(tokens, grad_keys),
                transposed_times(tokens, grad_values),
                transposed_times(grad_branch, attended),
                transposed_times(hidden_low, grad_pre),
                transposed_times(grad_mlp, activated),
            ],
            axis=1,
        ).astype(jnp.bfloat16),
        "shard",
        scatter_dimension=0,
        tiled=True,
    ).astype(jnp.float32)
    summed = lax.psum(summed.astype(jnp.bfloat16), "ctx").astype(jnp.float32)
    ff_half = up_full.shape[1]
    grad_query = summed[:, 0:half_width]
    grad_key = summed[:, half_width : 2 * half_width]
    grad_value = summed[:, 2 * half_width : 3 * half_width]
    grad_output = summed[:, 3 * half_width : 4 * half_width]
    grad_up = summed[:, 4 * half_width : 4 * half_width + ff_half]
    grad_down = summed[:, 4 * half_width + ff_half : 4 * half_width + 2 * ff_half]
    shard_index = lax.axis_index("shard")
    tp_index = lax.axis_index("tp")
    piece = DH // lax.axis_size("shard")
    heads_part = H // lax.axis_size("tp")
    grad_qv_bias = lax.dynamic_slice_in_dim(
        qv_total.reshape(2, heads_here, DH), shard_index * piece, piece, 2
    )
    grad_up_bias = lax.dynamic_slice_in_dim(
        up_total.reshape(ff_half // DH, DH), shard_index * piece, piece, 1
    )
    gain_rows = lax.dynamic_slice_in_dim(
        gain_total.reshape(2, H, DH), tp_index * heads_part, heads_part, 1
    )
    grad_gains = lax.dynamic_slice_in_dim(gain_rows, shard_index * piece, piece, 2)
    bias_rows = lax.dynamic_slice_in_dim(
        bias_total.reshape(4, H, DH), tp_index * heads_part, heads_part, 1
    )
    grad_biases = lax.dynamic_slice_in_dim(bias_rows, shard_index * piece, piece, 2)
    count_all = local_rows * lax.axis_size("shard") * lax.axis_size("ctx") * D
    root_squares = jnp.sqrt(square_total / count_all)
    outputs = result.astype(jnp.bfloat16).reshape(1, local_rows, D)
    input_out = input_grad.astype(jnp.bfloat16).reshape(1, local_rows, D)
    return (
        outputs,
        input_out,
        grad_query,
        grad_key,
        grad_value,
        grad_output,
        grad_up,
        grad_down,
        grad_qv_bias,
        grad_up_bias,
        grad_gains,
        grad_biases,
        root_squares,
    )


def solution(mesh):
    placed = (
        P("shard", "ctx", None),
        P("shard", "ctx", None),
        P("shard", "tp"),
        P("shard", "tp"),
        P("shard", "tp"),
        P("shard", "tp"),
        P("shard", "tp"),
        P("shard", "tp"),
        P(None, "tp", "shard"),
        P("tp", "shard"),
        P(None, "tp", "shard"),
        P(None, "tp", "shard"),
    )
    return jax.shard_map(
        shards,
        mesh=mesh,
        in_specs=placed,
        out_specs=(
            P("shard", "ctx", None),
            P("shard", "ctx", None),
            P("shard", "tp"),
            P("shard", "tp"),
            P("shard", "tp"),
            P("shard", "tp"),
            P("shard", "tp"),
            P("shard", "tp"),
            P(None, "tp", "shard"),
            P("tp", "shard"),
            P(None, "tp", "shard"),
            P(None, "tp", "shard"),
            P(),
        ),
        check_vma=False,
    )
```

profile of v0, /device:TPU:0, one launch (start us, length us, event | category | flops | bytes accessed | tf_op | source)
XLA Modules:
  0.0 2774.8 jit_solution(6751861890759885194)
XLA Ops:
  9.5 83.6 %all-gather.11.cloned.1.call-done = bf16[2048,1024]{1,0:T(8,128)(2,1)} async-done(((bf16[512,1024]{1,0:T(8,128)(2,1)}), bf16[2048,1024]{1,0:T(8,128)(2,1)}) %all-gather.11.cloned.1.call-update) | async-done | bytes 4194320 | tf_op jit(solution)/shard_map/all_gather | solution.py:98
  99.4 13.9 all_gather.43
  113.3 61.1 %all-gather.15.cloned.1.call-done = bf16[2048,1024]{1,0:T(8,128)(2,1)} async-done(((bf16[512,1024]{1,0:T(8,128)(2,1)}), bf16[2048,1024]{1,0:T(8,128)(2,1)}) %all-gather.15.cloned.1.call-update) | async-done | bytes 4194320 | tf_op jit(solution)/shard_map/all_gather | solution.py:99
  181.1 74.2 %all-gather.9.cloned.1.call-done = bf16[2048,1024]{1,0:T(8,128)(2,1)} async-done(((bf16[512,1024]{1,0:T(8,128)(2,1)}), bf16[2048,1024]{1,0:T(8,128)(2,1)}) %all-gather.9.cloned.1.call-update) | async-done | bytes 4194320 | tf_op jit(solution)/shard_map/all_gather | solution.py:97
  260.0 30.2 %all-gather.13.cloned.1.call-done = bf16[2048,1024]{1,0:T(8,128)(2,1)} async-done(((bf16[512,1024]{1,0:T(8,128)(2,1)}), bf16[2048,1024]{1,0:T(8,128)(2,1)}) %all-gather.13.cloned.1.call-update) | async-done | bytes 4194320 | tf_op jit(solution)/shard_map/all_gather | solution.py:119
  295.2 31.5 %all-gather.17.cloned.1.call-done = bf16[2048,1024]{1,0:T(8,128)(2,1)} async-done(((bf16[512,1024]{1,0:T(8,128)(2,1)}), bf16[2048,1024]{1,0:T(8,128)(2,1)}) %all-gather.17.cloned.1.call-update) | async-done | bytes 4194320 | tf_op jit(solution)/shard_map/all_gather | solution.py:120
  332.7 44.9 %while.26 = (s32[]{:T(128)}, bf16[8,512,128]{1,2,0:T(8,128)(2,1)}, f32[8,512]{1,0:T(8,128)S(1)}, bf16[8,512,128]{2,1,0:T(8,128)(2,1)S(1)}, bf16[8,2048,128]{2,1,...) while((s32[]{:T(128)}, bf16[8,512,128]{1,2,0:T(8,128)(2,1)}, ...), condition=%wide.region_3.4_spmd, body=%wide.region_0.3_spmd.sunk | while | flops 546307584 | bytes 14047329 | solution.py:125
  377.6 31.3 %all-gather.19.cloned.1.call-done = bf16[2048,1024]{1,0:T(8,128)(2,1)} async-done(((bf16[512,1024]{1,0:T(8,128)(2,1)}), bf16[2048,1024]{1,0:T(8,128)(2,1)}) %all-gather.19.cloned.1.call-update) | async-done | bytes 4194320 | tf_op jit(solution)/shard_map/all_gather | solution.py:100
  480.6 284.8 %all-gather.21.cloned.1.call-done = bf16[2048,4096]{1,0:T(8,128)(2,1)} async-done(((bf16[512,4096]{1,0:T(8,128)(2,1)}), bf16[2048,4096]{1,0:T(8,128)(2,1)}) %all-gather.21.cloned.1.call-update) | async-done | bytes 16777232 | tf_op jit(solution)/shard_map/all_gather | solution.py:133
  765.3 15.4 fusion.81
  780.7 271.1 %all-gather.23.cloned.1.call-done = bf16[2048,4096]{1,0:T(8,128)(2,1)} async-done(((bf16[512,4096]{1,0:T(8,128)(2,1)}), bf16[2048,4096]{1,0:T(8,128)(2,1)}) %all-gather.23.cloned.1.call-update) | async-done | bytes 16777232 | tf_op jit(solution)/shard_map/all_gather | solution.py:134
  1051.9 17.6 convolution_convert_fusion.3
  1069.8 61.1 %all-reduce.10.cloned.1.call-done = bf16[512,2048]{1,0:T(8,128)(2,1)} async-done(((bf16[512,2048]{1,0:T(8,128)(2,1)}), bf16[512,2048]{1,0:T(8,128)(2,1)}) %all-reduce.10.cloned.1.call-update) | async-done | bytes 2097168 | tf_op jit(solution)/shard_map/psum | solution.py:140
  1143.2 20.5 convert_reduce_fusion
  1179.1 63.0 %all-reduce.12.cloned.1.call-done = bf16[512,2048]{1,0:T(8,128)(2,1)} async-done(((bf16[512,2048]{1,0:T(8,128)(2,1)}), bf16[512,2048]{1,0:T(8,128)(2,1)}) %all-reduce.12.cloned.1.call-update) | async-done | bytes 2097168 | tf_op jit(solution)/shard_map/psum | solution.py:157
  1258.9 138.9 %while.27 = (s32[]{:T(128)}, bf16[8,512,128]{1,2,0:T(8,128)(2,1)}, bf16[8,2048,128]{1,2,0:T(8,128)(2,1)}, bf16[8,2048,128]{1,2,0:T(8,128)(2,1)}, bf16[8,512,128]...) while((s32[]{:T(128)}, bf16[8,512,128]{1,2,0:T(8,128)(2,1)}, ...), condition=%wide.region_17.18_spmd, body=%wide.region_15.17_spmd.sunk | while | flops 1351220736 | bytes 71447792 | solution.py:162
  1427.9 14.5 reduce-scatter.4.cloned.1.call-done
  1454.7 34.8 %reduce-scatter.6.cloned.1.call-done = bf16[512,1024]{0,1:T(8,128)(2,1)} async-done(((bf16[2048,1024]{0,1:T(8,128)(2,1)}), bf16[512,1024]{0,1:T(8,128)(2,1)}) %reduce-scatter.6.cloned.1.call-update) | async-done | bytes 1048592 | tf_op jit(solution)/shard_map/reduce_scatter | solution.py:170
  1512.5 15.4 convert_dynamic-update-slice_fusion.1
  1527.9 16.3 convert_dynamic-update-slice_fusion
  1567.3 797.9 %reduce-scatter.8.cloned.1.call-done = bf16[512,12288]{1,0:T(8,128)(2,1)} async-done(((bf16[2048,12288]{1,0:T(8,128)(2,1)}), bf16[512,12288]{1,0:T(8,128)(2,1)}) %reduce-scatter.8.cloned.1.call-update) | async-done | bytes 12582928 | tf_op jit(solution)/shard_map/reduce_scatter | solution.py:203
  2365.3 95.1 %all-reduce.18.cloned.1.call-done = (f32[2,8,128]{2,1,0:T(8,128)}, f32[32,128]{1,0:T(8,128)}, f32[2,16,128]{2,1,0:T(8,128)}, f32[4,16,128]{2,1,0:T(8,128)}, f32[3]{0:T(128)}) async-done(((f32[2,8,128]{2,1,0:T(8,128)}, f32[32,128]{1,0:T(8,128)}, f32[2,16,128]{2,1,0:T(8,128)}, f32[4,16,128]{2,1,0:T(8,128)}, f32[3]{0:T(128)}), (f32[2,8,128]{2,1,0:T(8,128)}, f32[32,128]{1,0:T(8,128)}, f32[2,16,128]{2,1,0:T(8,128)}, ...) | async-done | bytes 73756 | tf_op jit(solution)/shard_map/psum | solution.py:200
  2467.2 60.1 %all-reduce.14.cloned.1.call-done = bf16[512,2048]{1,0:T(8,128)(2,1)} async-done(((bf16[512,2048]{1,0:T(8,128)(2,1)}), bf16[512,2048]{1,0:T(8,128)(2,1)}) %all-reduce.14.cloned.1.call-update) | async-done | bytes 2097168 | tf_op jit(solution)/shard_map/psum | solution.py:181
  2532.1 218.1 %all-reduce.16.cloned.1.call-done = bf16[512,12288]{1,0:T(8,128)(2,1)} async-done(((bf16[512,12288]{1,0:T(8,128)(2,1)}), bf16[512,12288]{1,0:T(8,128)(2,1)}) %all-reduce.16.cloned.1.call-update) | async-done | bytes 12582928 | tf_op jit(solution)/shard_map/psum | solution.py:219
  (374 shorter events, 447.9 us)
Async XLA Ops:
  7.2 85.9 %all-gather.11.cloned.1.call-start = ((), (), s32[]{:S(2)}) async-start(), calls=%async_computation.4 | async-start | bytes 5242880 | tf_op jit(solution)/shard_map/all_gather | solution.py:98
  7.9 166.5 %all-gather.15.cloned.1.call-start = ((), (), s32[]{:S(2)}) async-start(), calls=%async_computation.6 | async-start | bytes 5242880 | tf_op jit(solution)/shard_map/all_gather | solution.py:99
  8.7 246.6 %all-gather.9.cloned.1.call-start = ((), (), s32[]{:S(2)}) async-start(), calls=%async_computation.3 | async-start | bytes 5242880 | tf_op jit(solution)/shard_map/all_gather | solution.py:97
  9.4 89.9 %copy-start.30 = (bf16[2,8,32]{2,1,0:T(8,128)(2,1)S(1)}, bf16[2,8,32]{2,1,0:T(8,128)(2,1)}, u32[]{:S(2)}) copy-start(bf16[2,8,32]{2,1,0:T(8,128)(2,1)} %param.24) | copy-start | bytes 3076
  9.4 165.0 %copy-start.1 = (bf16[1,512,2048]{2,1,0:T(8,128)(2,1)S(1)}, bf16[1,512,2048]{2,1,0:T(8,128)(2,1)}, u32[]{:S(2)}) copy-start(bf16[1,512,2048]{2,1,0:T(8,128)(2,1)} %param.16) | copy-start | bytes 6291460
  9.4 280.8 %all-gather.13.cloned.1.call-start = ((), (), s32[]{:S(2)}) async-start(), calls=%async_computation.5 | async-start | bytes 5242880 | tf_op jit(solution)/shard_map/all_gather | solution.py:119
  99.2 227.5 %all-gather.17.cloned.1.call-start = ((), (), s32[]{:S(2)}) async-start(), calls=%async_computation.7 | async-start | bytes 5242880 | tf_op jit(solution)/shard_map/all_gather | solution.py:120
  180.0 229.0 %all-gather.19.cloned.1.call-start = ((), (), s32[]{:S(2)}) async-start(), calls=%async_computation.8 | async-start | bytes 5242880 | tf_op jit(solution)/shard_map/all_gather | solution.py:100
  180.5 296.4 %all-reduce.8.cloned.1.call-start = ((), (), s32[]{:S(2)}) async-start(), calls=%async_computation.9 | async-start | bytes 4194304 | tf_op jit(solution)/shard_map/psum | solution.py:128
  415.2 19.8 copy-start.31
  415.2 37.5 %copy-start.29 = (bf16[32,32]{1,0:T(8,128)(2,1)S(1)}, bf16[32,32]{1,0:T(8,128)(2,1)}, u32[]{:S(2)}) copy-start(bf16[32,32]{1,0:T(8,128)(2,1)} %param.25) | copy-start | bytes 6148
  415.2 350.1 %all-gather.21.cloned.1.call-start = ((), (), s32[]{:S(2)}) async-start(), calls=%async_computation.10 | async-start | bytes 20971520 | tf_op jit(solution)/shard_map/all_gather | solution.py:133
  416.0 635.9 %all-gather.23.cloned.1.call-start = ((), (), s32[]{:S(2)}) async-start(), calls=%async_computation.11 | async-start | bytes 20971520 | tf_op jit(solution)/shard_map/all_gather | solution.py:134
  416.7 714.1 %all-reduce.10.cloned.1.call-start = ((), (), s32[]{:S(2)}) async-start(), calls=%async_computation.12 | async-start | bytes 4194304 | tf_op jit(solution)/shard_map/psum | solution.py:140
  466.2 664.7 %copy-start.24 = (f32[2048]{0:T(1024)}, f32[2048]{0:T(1024)S(1)}, u32[]{:S(2)}) copy-start(f32[2048]{0:T(1024)S(1)} %get-tuple-element.164) | copy-start | bytes 24580
  1069.5 172.7 %all-reduce.12.cloned.1.call-start = ((), (), s32[]{:S(2)}) async-start(), calls=%async_computation.13 | async-start | bytes 4194304 | tf_op jit(solution)/shard_map/psum | solution.py:157
  1143.2 20.5 copy-start.6
  1179.1 263.4 %reduce-scatter.4.cloned.1.call-start = ((), (), s32[]{:S(2)}) async-start(), calls=%async_computation.14 | async-start | bytes 5242880 | tf_op jit(solution)/shard_map/reduce_scatter | solution.py:167
  1397.9 91.5 %reduce-scatter.6.cloned.1.call-start = ((), (), s32[]{:S(2)}) async-start(), calls=%async_computation.15 | async-start | bytes 5242880 | tf_op jit(solution)/shard_map/reduce_scatter | solution.py:170
  1398.6 966.6 %reduce-scatter.8.cloned.1.call-start = ((), (), s32[]{:S(2)}) async-start(), calls=%async_computation.17 | async-start | bytes 62914560 | tf_op jit(solution)/shard_map/reduce_scatter | solution.py:203
  1512.5 15.4 copy-start.8
  1544.3 916.1 %all-reduce.18.cloned.1.call-start = ((), (), s32[]{:S(2)}) async-start(), calls=%async_computation.19 | async-start | bytes 148480 | tf_op jit(solution)/shard_map/psum | solution.py:200
  1558.4 968.9 %all-reduce.14.cloned.1.call-start = ((), (), s32[]{:S(2)}) async-start(), calls=%async_computation.16 | async-start | bytes 4194304 | tf_op jit(solution)/shard_map/psum | solution.py:181
  1567.3 1183.0 %all-reduce.16.cloned.1.call-start = ((), (), s32[]{:S(2)}) async-start(), calls=%async_computation.18 | async-start | bytes 25165824 | tf_op jit(solution)/shard_map/psum | solution.py:219
  (57 other events, 189.7 us)
Sparse Core Ops, SparseCore 0:
  9.6 83.4 all-gather.10
  94.6 79.7 all-gather.14
  176.0 79.2 all-gather.8
  257.3 32.9 all-gather.12
  292.2 34.4 all-gather.16
  328.1 80.7 all-gather.18
  415.3 61.6 all-reduce.7
  478.5 286.7 all-gather.20
  766.9 284.9 all-gather.22
  1069.6 61.1 all-reduce.9
  1179.2 62.9 all-reduce.11
  1398.0 44.3 reduce-scatter.3
  1445.0 44.3 reduce-scatter.5
  1544.4 820.7 reduce-scatter.7
  2370.3 90.0 all-reduce.17
  2463.1 64.0 all-reduce.13
  2529.6 220.6 all-reduce.15
where the time goes:
time: 2780 us; the launch traced here: 2770 us
  waiting for transfers between devices  2230 us (80%)
  matrix products  297 us (11%)
  local copies, waits for them, and re-layouts  124 us (4%)
  blocking collectives  62.7 us (2%)
  other arithmetic  46.4 us (2%)
    reduce_scatter x1, waiting for transfers between devices, shards(): lax.psum_scatter(jnp.concatenate([transposed_times(tokens, grad_queries),...  798 us
    all_gather x1, waiting for transfers between devices, shards(): lax.all_gather(up_weight, 'shard', axis=0, tiled=True)  285 us
    all_gather x1, waiting for transfers between devices, shards(): lax.all_gather(down_weight, 'shard', axis=0, tiled=True)  271 us
    psum x1, waiting for transfers between devices, shards(): summed = lax.psum(summed.astype(jnp.bfloat16), 'ctx').astype(jnp.float32)  218 us
    dot_general x30, matrix products, times_transposed(): lax.dot_general(left, right, (((1,), (1,)), ((), ())), preferred_element_...  104 us
    dot_general x22, matrix products, transposed_times(): lax.dot_general(left, right, (((0,), (0,)), ((), ())), preferred_element_...  101 us
    psum x1, waiting for transfers between devices, shards(): lax.psum((qv_sums, up_sums, gain_sums, bias_sums, square_sums), ('shard',...  95.1 us
    dot_general x22, matrix products, product(): return jnp.dot(left, right, preferred_element_type=jnp.float32)  91.5 us
  transfers between devices with their start and end apart: 17, of which 17 were waited for; matrix products, arithmetic and copies ran while one was open for 6% of the time, Pallas kernels for 0%

commit v1 on v0

--- a/solution.py
+++ b/solution.py
@@ -7,6 +7,19 @@
 H = 16
 DH = 128
 epsilon = 1e-12
+
+
+def gather_around(x, axis, dim):
+    ways = lax.axis_size(axis)
+    up = [(d, (d + 1) % ways) for d in range(ways)]
+    down = [(d, (d - 1) % ways) for d in range(ways)]
+    earlier, later = ([x], [x])
+    for _ in range(ways // 2):
+        earlier.append(lax.ppermute(earlier[-1], axis, up))
+    for _ in range((ways - 1) // 2):
+        later.append(lax.ppermute(later[-1], axis, down))
+    line = jnp.concatenate([*earlier[::-1], *later[1:]], axis=dim)
+    return jnp.roll(line, (lax.axis_index(axis) - ways // 2) * x.shape[dim], axis=dim)
 
 
 def product(left, right):
@@ -96,7 +109,7 @@
     gathered = (
         lax.all_gather(query_weight, "shard", axis=0, tiled=True),
         lax.all_gather(key_weight, "shard", axis=0, tiled=True),
-        lax.all_gather(value_weight, "shard", axis=0, tiled=True),
+        gather_around(value_weight, "shard", 0),
         lax.all_gather(output_weight, "shard", axis=0, tiled=True),
         lax.all_gather(query_value_bias, "shard", axis=2, tiled=True),
         lax.all_gather(norm_gains, "shard", axis=2, tiled=True),

time: 2780 us -> 2760 us (level)
  waiting for transfers between devices: 2230 us -> 2100 us
  blocking collectives: 62.7 us -> 138 us
    all_gather x1, waiting for transfers between devices: 83.6 us -> 0.02 us  [shards(): lax.all_gather(key_weight, 'shard', axis=0, tiled=True)]
    all_gather x1, blocking collectives: 13.9 us -> 88.8 us  [shards(): lax.all_gather(query_value_bias, 'shard', axis=2, tiled=True)]
    all_gather x1 -> x0, waiting for transfers between devices: 61.1 us -> none  [shards(): lax.all_gather(value_weight, 'shard', axis=0, tiled=True)]
    ppermute x0 -> x3, waiting for transfers between devices: none -> 38.4 us  [the longest x2 38.4 us: gather_around(): earlier.append(lax.ppermute(earlier[-1], axis, up))]
  transfers between devices with their start and end apart: 17 -> 19, of which waited for: 17 -> 16; matrix products, arithmetic and copies ran while one was open for 6% -> 6% of each run, Pallas kernels for 0% -> 0%
where the time goes in v1:
time: 2760 us; the launch traced here: 2750 us
  waiting for transfers between devices  2100 us (76%)
  matrix products  296 us (11%)
  blocking collectives  138 us (5%)
  local copies, waits for them, and re-layouts  135 us (5%)
  other arithmetic  46.3 us (2%)
    reduce_scatter x1, waiting for transfers between devices, shards(): lax.psum_scatter(jnp.concatenate([transposed_times(tokens, grad_queries),...  796 us
    all_gather x1, waiting for transfers between devices, shards(): lax.all_gather(up_weight, 'shard', axis=0, tiled=True)  285 us
    all_gather x1, waiting for transfers between devices, shards(): lax.all_gather(down_weight, 'shard', axis=0, tiled=True)  271 us
    psum x1, waiting for transfers between devices, shards(): summed = lax.psum(summed.astype(jnp.bfloat16), 'ctx').astype(jnp.float32)  218 us
    dot_general x30, matrix products, times_transposed(): lax.dot_general(left, right, (((1,), (1,)), ((), ())), preferred_element_...  106 us
    dot_general x22, matrix products, transposed_times(): lax.dot_general(left, right, (((0,), (0,)), ((), ())), preferred_element_...  101 us
    psum x1, waiting for transfers between devices, shards(): lax.psum((qv_sums, up_sums, gain_sums, bias_sums, square_sums), ('shard',...  95.2 us
    all_gather x1, blocking collectives, shards(): lax.all_gather(query_value_bias, 'shard', axis=2, tiled=True)  88.8 us
  transfers between devices with their start and end apart: 19, of which 16 were waited for; matrix products, arithmetic and copies ran while one was open for 6% of the time, Pallas kernels for 0%

profile of v1, /device:TPU:0, one launch (start us, length us, event | category | flops | bytes accessed | tf_op | source)
XLA Modules:
  0.0 2748.2 jit_solution(9740927569005020771)
XLA Ops:
  11.8 38.4 %collective-permute-done = bf16[512,1024]{1,0:T(8,128)(2,1)S(1)} collective-permute-done((bf16[512,1024]{1,0:T(8,128)(2,1)}, bf16[512,1024]{1,0:T(8,128)(2,1)S(1)}, u32[]{:S(2)}, u32[]{:S(2)}) %collective-permute-start) | collective-permute-done | bytes 1048608 | tf_op jit(solution)/shard_map/ppermute | solution.py:18
  50.2 15.0 collective-permute-start.1
  68.5 88.8 %all_gather.40 = bf16[2,8,128]{1,0,2:T(2,128)(2,1)S(1)} all-gather(bf16[2,8,32]{1,0,2:T(2,128)(2,1)S(1)} %copy.61), channel_id=1, replica_groups=mesh['shard'=4,'ctx'=4,'tp'=2] {'shard'}, dimensions={2}, use_global_device_ids=true | all-gather | bytes 5120 | tf_op jit(solution)/shard_map/all_gather | solution.py:114
  176.5 52.5 %all-gather.8.cloned.1.call-done = bf16[2048,1024]{1,0:T(8,128)(2,1)} async-done(((bf16[512,1024]{1,0:T(8,128)(2,1)}), bf16[2048,1024]{1,0:T(8,128)(2,1)}) %all-gather.8.cloned.1.call-update) | async-done | bytes 4194320 | tf_op jit(solution)/shard_map/all_gather | solution.py:110
  233.8 30.4 %all-gather.14.cloned.1.call-done = bf16[2048,1024]{0,1:T(8,128)(2,1)} async-done(((bf16[512,1024]{0,1:T(8,128)(2,1)}), bf16[2048,1024]{0,1:T(8,128)(2,1)}) %all-gather.14.cloned.1.call-update) | async-done | bytes 4194320 | tf_op jit(solution)/shard_map/all_gather | solution.py:133
  270.6 30.1 %all-gather.12.cloned.1.call-done = bf16[2048,1024]{1,0:T(8,128)(2,1)} async-done(((bf16[512,1024]{1,0:T(8,128)(2,1)}), bf16[2048,1024]{1,0:T(8,128)(2,1)}) %all-gather.12.cloned.1.call-update) | async-done | bytes 4194320 | tf_op jit(solution)/shard_map/all_gather | solution.py:132
  306.7 44.9 %while.26 = (s32[]{:T(128)}, bf16[8,512,128]{1,2,0:T(8,128)(2,1)}, f32[8,512]{1,0:T(8,128)S(1)}, bf16[8,512,128]{2,1,0:T(8,128)(2,1)S(1)}, bf16[8,2048,128]{2,1,...) while((s32[]{:T(128)}, bf16[8,512,128]{1,2,0:T(8,128)(2,1)}, ...), condition=%wide.region_3.4_spmd, body=%wide.region_0.3_spmd.sunk | while | flops 546307584 | bytes 14047329 | solution.py:138
  351.6 31.2 %all-gather.16.cloned.1.call-done = bf16[2048,1024]{1,0:T(8,128)(2,1)} async-done(((bf16[512,1024]{1,0:T(8,128)(2,1)}), bf16[2048,1024]{1,0:T(8,128)(2,1)}) %all-gather.16.cloned.1.call-update) | async-done | bytes 4194320 | tf_op jit(solution)/shard_map/all_gather | solution.py:113
  454.5 284.8 %all-gather.18.cloned.1.call-done = bf16[2048,4096]{1,0:T(8,128)(2,1)} async-done(((bf16[512,4096]{1,0:T(8,128)(2,1)}), bf16[2048,4096]{1,0:T(8,128)(2,1)}) %all-gather.18.cloned.1.call-update) | async-done | bytes 16777232 | tf_op jit(solution)/shard_map/all_gather | solution.py:146
  739.3 15.4 fusion.93
  754.6 271.2 %all-gather.20.cloned.1.call-done = bf16[2048,4096]{1,0:T(8,128)(2,1)} async-done(((bf16[512,4096]{1,0:T(8,128)(2,1)}), bf16[2048,4096]{1,0:T(8,128)(2,1)}) %all-gather.20.cloned.1.call-update) | async-done | bytes 16777232 | tf_op jit(solution)/shard_map/all_gather | solution.py:147
  1025.8 17.6 convolution_convert_fusion.3
  1043.7 61.1 %all-reduce.10.cloned.1.call-done = bf16[512,2048]{1,0:T(8,128)(2,1)} async-done(((bf16[512,2048]{1,0:T(8,128)(2,1)}), bf16[512,2048]{1,0:T(8,128)(2,1)}) %all-reduce.10.cloned.1.call-update) | async-done | bytes 2097168 | tf_op jit(solution)/shard_map/psum | solution.py:153
  1117.1 20.5 convert_reduce_fusion
  1153.1 63.1 %all-reduce.12.cloned.1.call-done = bf16[512,2048]{1,0:T(8,128)(2,1)} async-done(((bf16[512,2048]{1,0:T(8,128)(2,1)}), bf16[512,2048]{1,0:T(8,128)(2,1)}) %all-reduce.12.cloned.1.call-update) | async-done | bytes 2097168 | tf_op jit(solution)/shard_map/psum | solution.py:170
  1232.7 138.9 %while.27 = (s32[]{:T(128)}, bf16[8,512,128]{1,2,0:T(8,128)(2,1)}, bf16[8,2048,128]{1,2,0:T(8,128)(2,1)}, bf16[8,2048,128]{1,2,0:T(8,128)(2,1)}, bf16[8,512,128]...) while((s32[]{:T(128)}, bf16[8,512,128]{1,2,0:T(8,128)(2,1)}, ...), condition=%wide.region_17.18_spmd, body=%wide.region_15.17_spmd.sunk | while | flops 1351220736 | bytes 71447792 | solution.py:175
  1401.7 14.5 reduce-scatter.4.cloned.1.call-done
  1428.5 34.6 %reduce-scatter.6.cloned.1.call-done = bf16[512,1024]{0,1:T(8,128)(2,1)} async-done(((bf16[2048,1024]{0,1:T(8,128)(2,1)}), bf16[512,1024]{0,1:T(8,128)(2,1)}) %reduce-scatter.6.cloned.1.call-update) | async-done | bytes 1048592 | tf_op jit(solution)/shard_map/reduce_scatter | solution.py:183
  1486.2 15.3 convert_dynamic-update-slice_fusion.1
  1501.4 16.2 convert_dynamic-update-slice_fusion
  1543.0 795.7 %reduce-scatter.8.cloned.1.call-done = bf16[512,12288]{1,0:T(8,128)(2,1)} async-done(((bf16[2048,12288]{1,0:T(8,128)(2,1)}), bf16[512,12288]{1,0:T(8,128)(2,1)}) %reduce-scatter.8.cloned.1.call-update) | async-done | bytes 12582928 | tf_op jit(solution)/shard_map/reduce_scatter | solution.py:216
  2338.7 95.2 %all-reduce.18.cloned.1.call-done = (f32[2,8,128]{2,1,0:T(8,128)}, f32[32,128]{1,0:T(8,128)}, f32[2,16,128]{2,1,0:T(8,128)}, f32[4,16,128]{2,1,0:T(8,128)}, f32[3]{0:T(128)}) async-done(((f32[2,8,128]{2,1,0:T(8,128)}, f32[32,128]{1,0:T(8,128)}, f32[2,16,128]{2,1,0:T(8,128)}, f32[4,16,128]{2,1,0:T(8,128)}, f32[3]{0:T(128)}), (f32[2,8,128]{2,1,0:T(8,128)}, f32[32,128]{1,0:T(8,128)}, f32[2,16,128]{2,1,0:T(8,128)}, ...) | async-done | bytes 73756 | tf_op jit(solution)/shard_map/psum | solution.py:213
  2440.6 60.1 %all-reduce.14.cloned.1.call-done = bf16[512,2048]{1,0:T(8,128)(2,1)} async-done(((bf16[512,2048]{1,0:T(8,128)(2,1)}), bf16[512,2048]{1,0:T(8,128)(2,1)}) %all-reduce.14.cloned.1.call-update) | async-done | bytes 2097168 | tf_op jit(solution)/shard_map/psum | solution.py:194
  2505.6 218.1 %all-reduce.16.cloned.1.call-done = bf16[512,12288]{1,0:T(8,128)(2,1)} async-done(((bf16[512,12288]{1,0:T(8,128)(2,1)}), bf16[512,12288]{1,0:T(8,128)(2,1)}) %all-reduce.16.cloned.1.call-update) | async-done | bytes 12582928 | tf_op jit(solution)/shard_map/psum | solution.py:232
  (385 shorter events, 463.4 us)
Async XLA Ops:
  7.2 151.7 %copy-start.16 = (bf16[512,1024]{1,0:T(8,128)(2,1)S(1)}, bf16[512,1024]{1,0:T(8,128)(2,1)}, u32[]{:S(2)}) copy-start(bf16[512,1024]{1,0:T(8,128)(2,1)} %param.20) | copy-start | bytes 3145732
  7.2 162.6 %all-gather.10.cloned.1.call-start = ((), (), s32[]{:S(2)}) async-start(), calls=%async_computation.4 | async-start | bytes 5242880 | tf_op jit(solution)/shard_map/all_gather | solution.py:111
  7.9 221.1 %all-gather.8.cloned.1.call-start = ((), (), s32[]{:S(2)}) async-start(), calls=%async_computation.3 | async-start | bytes 5242880 | tf_op jit(solution)/shard_map/all_gather | solution.py:110
  8.7 255.5 %all-gather.14.cloned.1.call-start = ((), (), s32[]{:S(2)}) async-start(), calls=%async_computation.6 | async-start | bytes 5242880 | tf_op jit(solution)/shard_map/all_gather | solution.py:133
  8.7 41.5 %collective-permute-start = (bf16[512,1024]{1,0:T(8,128)(2,1)}, bf16[512,1024]{1,0:T(8,128)(2,1)S(1)}, u32[]{:S(2)}, u32[]{:S(2)}) collective-permute-start(bf16[512,1024]{1,0:T(8,128)(2,1)} %param.20), channel_id=1, source_target_pairs={{0,8},{8,16},{16,24},{24,0},{1,9},{9,17},{17,25},{25,1},{2,10},{10... | collective-permute-start | bytes 3145736 | tf_op jit(solution)/shard_map/ppermute | solution.py:18
  50.2 108.8 %copy-start.17 = (bf16[512,1024]{1,0:T(8,128)(2,1)}, bf16[512,1024]{1,0:T(8,128)(2,1)S(1)}, u32[]{:S(2)}) copy-start(bf16[512,1024]{1,0:T(8,128)(2,1)S(1)} %collective-permute-done) | copy-start | bytes 3145732
  50.2 107.2 %collective-permute-start.1 = (bf16[512,1024]{1,0:T(8,128)(2,1)S(1)}, bf16[512,1024]{1,0:T(8,128)(2,1)}, u32[]{:S(2)}, u32[]{:S(2)}) collective-permute-start(bf16[512,1024]{1,0:T(8,128)(2,1)S(1)} %collective-permute-done), channel_id=1, source_target_pairs={{0,8},{8,16},{16,24},{24,0},{1,9},{9,17},{17,25},{25,1},{2,10},{10... | collective-permute-start | bytes 3145736 | tf_op jit(solution)/shard_map/ppermute | solution.py:18
  65.2 93.8 %collective-permute-start.2 = (bf16[512,1024]{1,0:T(8,128)(2,1)}, bf16[512,1024]{1,0:T(8,128)(2,1)S(1)}, u32[]{:S(2)}, u32[]{:S(2)}) collective-permute-start(bf16[512,1024]{1,0:T(8,128)(2,1)} %param.20), channel_id=1, source_target_pairs={{0,24},{8,0},{16,8},{24,16},{1,25},{9,1},{17,9},{25,17},{2,26},{10... | collective-permute-start | bytes 3145736 | tf_op jit(solution)/shard_map/ppermute | solution.py:20
  169.8 130.9 %all-gather.12.cloned.1.call-start = ((), (), s32[]{:S(2)}) async-start(), calls=%async_computation.5 | async-start | bytes 5242880 | tf_op jit(solution)/shard_map/all_gather | solution.py:132
  175.4 207.5 %all-gather.16.cloned.1.call-start = ((), (), s32[]{:S(2)}) async-start(), calls=%async_computation.7 | async-start | bytes 5242880 | tf_op jit(solution)/shard_map/all_gather | solution.py:113
  176.0 274.9 %all-reduce.8.cloned.1.call-start = ((), (), s32[]{:S(2)}) async-start(), calls=%async_computation.8 | async-start | bytes 4194304 | tf_op jit(solution)/shard_map/psum | solution.py:141
  389.1 37.5 %copy-start.31 = (bf16[32,32]{1,0:T(8,128)(2,1)S(1)}, bf16[32,32]{1,0:T(8,128)(2,1)}, u32[]{:S(2)}) copy-start(bf16[32,32]{1,0:T(8,128)(2,1)} %param.25) | copy-start | bytes 6148
  389.1 350.1 %all-gather.18.cloned.1.call-start = ((), (), s32[]{:S(2)}) async-start(), calls=%async_computation.9 | async-start | bytes 20971520 | tf_op jit(solution)/shard_map/all_gather | solution.py:146
  389.9 635.9 %all-gather.20.cloned.1.call-start = ((), (), s32[]{:S(2)}) async-start(), calls=%async_computation.10 | async-start | bytes 20971520 | tf_op jit(solution)/shard_map/all_gather | solution.py:147
  390.6 714.1 %all-reduce.10.cloned.1.call-start = ((), (), s32[]{:S(2)}) async-start(), calls=%async_computation.11 | async-start | bytes 4194304 | tf_op jit(solution)/shard_map/psum | solution.py:153
  440.1 664.7 %copy-start.26 = (f32[2048]{0:T(1024)}, f32[2048]{0:T(1024)S(1)}, u32[]{:S(2)}) copy-start(f32[2048]{0:T(1024)S(1)} %get-tuple-element.164) | copy-start | bytes 24580
  1043.4 172.7 %all-reduce.12.cloned.1.call-start = ((), (), s32[]{:S(2)}) async-start(), calls=%async_computation.12 | async-start | bytes 4194304 | tf_op jit(solution)/shard_map/psum | solution.py:170
  1117.1 20.5 copy-start.6
  1153.0 263.2 %reduce-scatter.4.cloned.1.call-start = ((), (), s32[]{:S(2)}) async-start(), calls=%async_computation.13 | async-start | bytes 5242880 | tf_op jit(solution)/shard_map/reduce_scatter | solution.py:180
  1371.7 91.4 %reduce-scatter.6.cloned.1.call-start = ((), (), s32[]{:S(2)}) async-start(), calls=%async_computation.14 | async-start | bytes 5242880 | tf_op jit(solution)/shard_map/reduce_scatter | solution.py:183
  1372.3 966.4 %reduce-scatter.8.cloned.1.call-start = ((), (), s32[]{:S(2)}) async-start(), calls=%async_computation.16 | async-start | bytes 62914560 | tf_op jit(solution)/shard_map/reduce_scatter | solution.py:216
  1517.7 916.1 %all-reduce.18.cloned.1.call-start = ((), (), s32[]{:S(2)}) async-start(), calls=%async_computation.18 | async-start | bytes 148480 | tf_op jit(solution)/shard_map/psum | solution.py:213
  1531.9 968.8 %all-reduce.14.cloned.1.call-start = ((), (), s32[]{:S(2)}) async-start(), calls=%async_computation.15 | async-start | bytes 4194304 | tf_op jit(solution)/shard_map/psum | solution.py:194
  1542.9 1180.8 %all-reduce.16.cloned.1.call-start = ((), (), s32[]{:S(2)}) async-start(), calls=%async_computation.17 | async-start | bytes 25165824 | tf_op jit(solution)/shard_map/psum | solution.py:232
  (59 other events, 205.0 us)
Sparse Core Ops, SparseCore 0:
  9.6 138.9 all-gather.9
  150.1 78.9 all-gather.7
  231.2 32.9 all-gather.13
  266.1 34.4 all-gather.11
  302.1 80.7 all-gather.15
  389.2 61.6 all-reduce.7
  452.5 286.7 all-gather.17
  740.8 284.9 all-gather.19
  1043.5 61.1 all-reduce.9
  1153.1 62.9 all-reduce.11
  1371.8 44.3 reduce-scatter.3
  1418.6 44.3 reduce-scatter.5
  1517.8 820.7 reduce-scatter.7
  2343.8 90.0 all-reduce.17
  2436.6 64.0 all-reduce.13
  2503.0 220.6 all-reduce.15
